TPU v7x, 32 devices: a whole 2x2x4 slice. The times are simulated.
32 devices in a mesh: dap: 32 (over z, y, x, core).
Axes of the slice: x: 2, y: 2, z: 4, core: 2. Of those that a mesh axis runs over, the one named last changes fastest.
Arguments:
- homolog_stack: float32 [64, 64, 256], P('dap'), may hold values from -5 to 5
- couple_tensor: float32 [64, 64, 128], P('dap'), may hold values from -6 to 6
- homolog_presence: int32 [64, 64], P('dap'), may hold values from 0 to 1
- amino_presence: int32 [64], replicated, may hold values 0 or 1
- horizontal_standard_factor: float32 [256], replicated, may hold values from 0.5 to 1.5
- horizontal_asking_matrix: bfloat16 [256, 256], replicated, may hold values from -7 to 7
- horizontal_lookup_triple: bfloat16 [256, 768], replicated, may hold values from -0.375 to 0.375
- horizontal_final_matrix: bfloat16 [256, 256], replicated, may hold values from -0.375 to 0.375
- couple_offset_factor: float32 [128], replicated, may hold values from 0.5 to 1.5
- couple_offset_matrix: bfloat16 [128, 8], replicated, may hold values from -2 to 2
- vertical_standard_factor: float32 [256], replicated, may hold values from 0.5 to 1.5
- vertical_asking_matrix: bfloat16 [256, 256], replicated, may hold values from -7 to 7
- vertical_lookup_triple: bfloat16 [256, 768], replicated, may hold values from -0.375 to 0.375
- vertical_final_matrix: bfloat16 [256, 256], replicated, may hold values from -0.375 to 0.375
- tensor_average_factor: float32 [256], replicated, may hold values from 0.5 to 1.5
- tensor_average_mapping: bfloat16 [256, 64], replicated, may hold values from -0.375 to 0.375
- tensor_average_final: bfloat16 [1024, 128], replicated, may hold values from -0.375 to 0.375
- trio_entry_factors: float32 [2, 128], replicated, may hold values from 0.5 to 1.5
- trio_flank_mappings: bfloat16 [2, 128, 512], replicated, may hold values from -0.5 to 0.5
- trio_final_switches: bfloat16 [2, 128, 128], replicated, may hold values from -0.5 to 0.5
- trio_multiplied_factors: float32 [2, 128], replicated, may hold values from 0.5 to 1.5
- trio_final_matrices: bfloat16 [2, 128, 128], replicated, may hold values from -1 to 1
Outputs:
- msa_out: float32 [64, 64, 256], P(None, 'dap')
- pair_out: float32 [64, 64, 128], P('dap')
All inputs are finite; a program needn't handle non-finite values.
Results may differ from a plain program's by a relative error of at most 0.015.
Values may be sent and summed in bfloat16 or wider, within the bound.
No kernel may reach another device: no remote copies, remote signals or barrier semaphores. Data moves between devices by JAX's collectives and lax.ppermute only.
A program may use at most 64 MiB of HBM per device.

v0:
```python
import math
import jax
import jax.numpy as jnp
from jax import lax
from jax.sharding import PartitionSpec as P

FOCUS_NUMBER = 8
PER_FOCUS_WIDTH = 32
TENSOR_HIDDEN = 32
TRI_HID = 128
EPSILON = 1e-05
MASK_PENALTY_SCALE = 1000000000.0


def standardize_features(content_vectors, gain, axis):
    centred = content_vectors - jnp.mean(content_vectors, axis=axis, keepdims=True)
    spread = jnp.mean(centred * centred, axis=axis, keepdims=True)
    return centred * lax.rsqrt(spread + EPSILON) * gain


def triangle(
    pair_now, gain_in, proj_weight, gate_weight, gain_mid, final_weight, amino_presence, incoming
):
    hidden = TRI_HID
    row_count = pair_now.shape[0]
    my_index = lax.axis_index("dap")
    standardized_source = standardize_features(pair_now, gain_in, -1).astype(jnp.bfloat16)
    projected = jnp.einsum(
        "rkd,de->erk", standardized_source, proj_weight, preferred_element_type=jnp.float32
    )
    res_float = amino_presence.astype(jnp.float32)
    own_rows = lax.dynamic_slice_in_dim(res_float, my_index * row_count, row_count)
    pair_mask = own_rows[:, None] * res_float[None, :]
    left_side = (
        jax.nn.sigmoid(projected[hidden : 2 * hidden]) * projected[:hidden] * pair_mask[None]
    ).astype(jnp.bfloat16)
    right_side = (
        jax.nn.sigmoid(projected[3 * hidden :])
        * projected[2 * hidden : 3 * hidden]
        * pair_mask[None]
    ).astype(jnp.bfloat16)
    gating = jax.nn.sigmoid(
        jnp.dot(standardized_source, gate_weight, preferred_element_type=jnp.float32)
    )
    left_chan, right_chan = (
        lax.all_to_all(left_side, "dap", split_axis=0, concat_axis=1, tiled=True),
        lax.all_to_all(right_side, "dap", split_axis=0, concat_axis=1, tiled=True),
    )
    if incoming:
        product = jnp.einsum(
            "cki,ckj->cij", left_chan, right_chan, preferred_element_type=jnp.float32
        )
    else:
        product = jnp.einsum(
            "cik,cjk->cij", left_chan, right_chan, preferred_element_type=jnp.float32
        )
    product = product.astype(jnp.bfloat16)
    returned = lax.all_to_all(product, "dap", split_axis=1, concat_axis=0, tiled=True)
    product_normed = standardize_features(
        returned.astype(jnp.float32), gain_mid[:, None, None], 0
    ).astype(jnp.bfloat16)
    update = jnp.einsum(
        "crj,cd->rjd", product_normed, final_weight, preferred_element_type=jnp.float32
    )
    return pair_now + update * gating


def shards(
    homolog_stack,
    couple_tensor,
    homolog_presence,
    amino_presence,
    horizontal_standard_factor,
    horizontal_asking_matrix,
    horizontal_lookup_triple,
    horizontal_final_matrix,
    couple_offset_factor,
    couple_offset_matrix,
    vertical_standard_factor,
    vertical_asking_matrix,
    vertical_lookup_triple,
    vertical_final_matrix,
    tensor_average_factor,
    tensor_average_mapping,
    tensor_average_final,
    trio_entry_factors,
    trio_flank_mappings,
    trio_final_switches,
    trio_multiplied_factors,
    trio_final_matrices,
):
    nested_function = FOCUS_NUMBER * PER_FOCUS_WIDTH
    scaling = 1.0 / math.sqrt(PER_FOCUS_WIDTH)
    strand_portion = homolog_stack.shape[0]
    amino_total = homolog_stack.shape[1]
    row_count = couple_tensor.shape[0]
    pair_normed = standardize_features(couple_tensor, couple_offset_factor, -1).astype(jnp.bfloat16)
    bias_local = jnp.einsum(
        "rjc,ch->hrj", pair_normed, couple_offset_matrix, preferred_element_type=jnp.float32
    ).astype(jnp.bfloat16)
    standardized_source = standardize_features(
        homolog_stack, horizontal_standard_factor, -1
    ).astype(jnp.bfloat16)
    shaped = (strand_portion, amino_total, FOCUS_NUMBER, PER_FOCUS_WIDTH)
    queries = (
        (
            jnp.dot(
                standardized_source, horizontal_asking_matrix, preferred_element_type=jnp.float32
            )
            * scaling
        )
        .astype(jnp.bfloat16)
        .reshape(shaped)
    )
    others = jnp.dot(
        standardized_source, horizontal_lookup_triple, preferred_element_type=jnp.float32
    )
    keys_all = others[..., :nested_function].astype(jnp.bfloat16).reshape(shaped)
    content_entire = (
        others[..., nested_function : 2 * nested_function].astype(jnp.bfloat16).reshape(shaped)
    )
    sigmoid_switches = jax.nn.sigmoid(others[..., 2 * nested_function :])
    mask_penalty = MASK_PENALTY_SCALE * (homolog_presence.astype(jnp.float32) - 1.0)

    def attend(bias_piece):
        query_rows = bias_piece.shape[1]
        scores = jnp.einsum(
            "sihc,sjhc->shij", queries, keys_all, preferred_element_type=jnp.float32
        )
        scores = scores + bias_piece.astype(jnp.float32)[None] + mask_penalty[:, None, None, :]
        softmax_probabilities = jax.nn.softmax(scores, axis=-1).astype(jnp.bfloat16)
        mixed = jnp.einsum(
            "shij,sjhc->sihc",
            softmax_probabilities,
            content_entire,
            preferred_element_type=jnp.float32,
        )
        return mixed.reshape(strand_portion, query_rows, nested_function)

    bias_whole = lax.all_gather(bias_local, "dap", axis=1, tiled=True)
    block_rows = math.gcd(amino_total, 256)

    def one_block(block_index):
        return attend(bias_whole)

    blocks = lax.map(one_block, jnp.arange(amino_total // block_rows, dtype=jnp.int32))
    focused_content = jnp.moveaxis(blocks, 0, 1).reshape(
        strand_portion, amino_total, nested_function
    )
    homolog_stack_horizontal = homolog_stack + jnp.dot(
        (focused_content * sigmoid_switches).astype(jnp.bfloat16),
        horizontal_final_matrix,
        preferred_element_type=jnp.float32,
    )
    column_view, col_mask = (
        lax.all_to_all(
            homolog_stack_horizontal.astype(jnp.bfloat16),
            "dap",
            split_axis=1,
            concat_axis=0,
            tiled=True,
        ).astype(homolog_stack_horizontal.dtype),
        lax.all_to_all(
            homolog_presence.astype(jnp.float32).astype(jnp.bfloat16),
            "dap",
            split_axis=1,
            concat_axis=0,
            tiled=True,
        ).astype(jnp.float32),
    )
    seq_total = column_view.shape[0]
    col_shape = (seq_total, row_count, FOCUS_NUMBER, PER_FOCUS_WIDTH)
    standardized_source = standardize_features(column_view, vertical_standard_factor, -1).astype(
        jnp.bfloat16
    )
    col_queries = (
        (
            jnp.dot(standardized_source, vertical_asking_matrix, preferred_element_type=jnp.float32)
            * scaling
        )
        .astype(jnp.bfloat16)
        .reshape(col_shape)
    )
    col_others = jnp.dot(
        standardized_source, vertical_lookup_triple, preferred_element_type=jnp.float32
    )
    col_keys = col_others[..., :nested_function].astype(jnp.bfloat16).reshape(col_shape)
    col_values = (
        col_others[..., nested_function : 2 * nested_function]
        .astype(jnp.bfloat16)
        .reshape(col_shape)
    )
    col_gates = jax.nn.sigmoid(col_others[..., 2 * nested_function :])
    col_penalty = MASK_PENALTY_SCALE * (col_mask - 1.0)
    scores = jnp.einsum(
        "sihc,tihc->ihst", col_queries, col_keys, preferred_element_type=jnp.float32
    )
    scores = scores + jnp.transpose(col_penalty)[:, None, None, :]
    softmax_probabilities = jax.nn.softmax(scores, axis=-1).astype(jnp.bfloat16)
    col_mixed = jnp.einsum(
        "uovg,guox->vuox", softmax_probabilities, col_values, preferred_element_type=jnp.float32
    ).reshape(seq_total, row_count, nested_function)
    alignment_after_columns = column_view + jnp.dot(
        (col_mixed * col_gates).astype(jnp.bfloat16),
        vertical_final_matrix,
        preferred_element_type=jnp.float32,
    )
    standardized_source = standardize_features(
        alignment_after_columns, tensor_average_factor, -1
    ).astype(jnp.bfloat16)
    halves = jnp.dot(
        standardized_source, tensor_average_mapping, preferred_element_type=jnp.float32
    )
    left_proj = (halves[..., :TENSOR_HIDDEN] * col_mask[..., None]).astype(jnp.bfloat16)
    right_proj = (halves[..., TENSOR_HIDDEN:] * col_mask[..., None]).astype(jnp.bfloat16)
    right_whole, mask_whole = (
        lax.all_gather(right_proj, "dap", axis=1, tiled=True),
        lax.all_gather(col_mask.astype(jnp.bfloat16), "dap", axis=1, tiled=True),
    )
    outer = jnp.einsum("sra,sjb->rjab", left_proj, right_whole, preferred_element_type=jnp.float32)
    outer = outer.astype(jnp.bfloat16).reshape(
        row_count, amino_total, TENSOR_HIDDEN * TENSOR_HIDDEN
    )
    counts = jnp.dot(
        jnp.transpose(col_mask), mask_whole.astype(jnp.float32), precision=lax.Precision.HIGHEST
    )
    product = (
        jnp.dot(outer, tensor_average_final, preferred_element_type=jnp.float32)
        / jnp.maximum(counts, 1.0)[..., None]
    )
    pair_one = couple_tensor + product
    pair_two = triangle(
        pair_one,
        trio_entry_factors[0],
        trio_flank_mappings[0],
        trio_final_switches[0],
        trio_multiplied_factors[0],
        trio_final_matrices[0],
        amino_presence,
        False,
    )
    pair_after_incoming = triangle(
        pair_two,
        trio_entry_factors[1],
        trio_flank_mappings[1],
        trio_final_switches[1],
        trio_multiplied_factors[1],
        trio_final_matrices[1],
        amino_presence,
        True,
    )
    return (alignment_after_columns, pair_after_incoming)


def solution(mesh):
    placed = (
        P("dap", None, None),
        P("dap", None, None),
        P("dap", None),
        P(),
        P(),
        P(),
        P(),
        P(),
        P(),
        P(),
        P(),
        P(),
        P(),
        P(),
        P(),
        P(),
        P(),
        P(),
        P(),
        P(),
        P(),
        P(),
    )
    return jax.shard_map(
        shards,
        mesh=mesh,
        in_specs=placed,
        out_specs=(P(None, "dap", None), P("dap", None, None)),
        check_vma=False,
    )
```

profile of v0, /device:TPU:0, one launch (start us, length us, event | category | flops | bytes accessed | tf_op | source)
XLA Modules:
  0.0 221.2 jit_solution(10079408757036569126)
XLA Ops:
  0.7 0.8 convert_convert_fusion
  1.5 0.6 copy.137
  2.2 7.3 %all-to-all-start.1 = ((bf16[2,32,2]{2,0,1:T(2,128)(2,1)}), bf16[2,32,2]{2,0,1:T(2,128)(2,1)S(1)}, u32[]{:S(2)}, u32[]{:S(2)}) async-start(bf16[2,32,2]{2,0,1:T(2,128)(2,1)} %copy.137), calls=%async_computation.1 | async-start | bytes 32768 | tf_op jit(solution)/shard_map/all_to_all | solution.py:163
  9.5 0.7 add_multiply_fusion
  10.2 1.0 reduce_sum.163
  11.4 0.7 copy-done.10
  12.5 0.8 copy-done.6
  13.6 0.7 copy-done.2
  14.6 0.5 copy-done.18
  15.5 42.1 %all_gather.9 = bf16[8,64,64]{2,0,1:T(8,128)(2,1)S(1)} all-gather(bf16[8,2,64]{2,0,1:T(8,128)(2,1)S(1)} %fusion.22), channel_id=1, replica_groups=mesh['dap'=32] {'dap'}, dimensions={1}, use_global_device_ids=true | all-gather | bytes 67584 | tf_op jit(solution)/shard_map/all_gather | solution.py:140
  58.0 0.4 fusion.118
  58.9 0.5 copy-done.13
  59.5 0.7 copy-done.20
  60.5 0.7 copy.126
  61.2 2.6 %all-to-all-start = ((bf16[2,64,256]{2,0,1:T(2,128)(2,1)}), bf16[2,64,256]{2,0,1:T(2,128)(2,1)S(1)}, u32[]{:S(2)}, u32[]{:S(2)}) async-start(bf16[2,64,256]{2,0,1:T(2,128)(2,1)} %copy.126), calls=%async_computation | async-start | bytes 131072 | tf_op jit(solution)/shard_map/all_to_all | solution.py:156
  63.8 41.8 %all-gather = bf16[32,2,64]{2,1,0:T(2,128)(2,1)S(1)} all-gather(bf16[1,2,64]{2,1,0:T(2,128)(2,1)S(1)} %bitcast.220), channel_id=1, replica_groups=mesh['dap'=32] {'dap'}, dimensions={0}, use_global_device_ids=true | all-gather | bytes 8448 | tf_op jit(solution)/shard_map/all_gather | solution.py:218
  107.3 0.6 copy-done.11
  108.3 0.8 copy-done.7
  109.7 0.4 fusion.120
  110.6 0.8 copy-done.16
  111.9 0.6 copy-done.9
  112.8 38.1 %all_gather.10 = bf16[64,64,32]{0,2,1:T(8,128)(2,1)S(1)} all-gather(bf16[64,2,32]{0,2,1:T(8,128)(2,1)S(1)} %fusion.80), channel_id=1, replica_groups=mesh['dap'=32] {'dap'}, dimensions={1}, use_global_device_ids=true | all-gather | bytes 270336 | tf_op jit(solution)/shard_map/all_gather | solution.py:217
  150.9 0.6 fusion.6
  151.9 0.6 copy-done.4
  152.5 0.4 fusion.122
  153.0 0.4 copy-done.5
  153.9 0.7 reshape.256
  154.6 2.6 %all-to-all-start.2 = ((bf16[32,2,256]{2,1,0:T(2,128)(2,1)}), bf16[32,2,256]{2,1,0:T(2,128)(2,1)S(1)}, u32[]{:S(2)}, u32[]{:S(2)}) async-start(bf16[32,2,256]{2,1,0:T(2,128)(2,1)} %reshape.256), calls=%async_computation.2 | async-start | bytes 65536 | tf_op jit(solution)/shard_map/all_to_all | solution.py:46
  157.3 0.7 reshape.258
  158.0 6.4 %all-to-all-done.2 = bf16[32,2,256]{2,1,0:T(2,128)(2,1)S(1)} async-done(((bf16[32,2,256]{2,1,0:T(2,128)(2,1)}), bf16[32,2,256]{2,1,0:T(2,128)(2,1)S(1)}, u32[]{:S(2)}, u32[]{:S(2)}) %all-to-all-start.2) | async-done | bytes 32800 | tf_op jit(solution)/shard_map/all_to_all | solution.py:46
  164.4 2.6 %all-to-all-start.3 = ((bf16[32,2,256]{2,1,0:T(2,128)(2,1)}), bf16[32,2,256]{2,1,0:T(2,128)(2,1)S(1)}, u32[]{:S(2)}, u32[]{:S(2)}) async-start(bf16[32,2,256]{2,1,0:T(2,128)(2,1)} %reshape.258), calls=%async_computation.3 | async-start | bytes 65536 | tf_op jit(solution)/shard_map/all_to_all | solution.py:47
  167.2 7.0 %all-to-all-done.3 = bf16[32,2,256]{2,1,0:T(2,128)(2,1)S(1)} async-done(((bf16[32,2,256]{2,1,0:T(2,128)(2,1)}), bf16[32,2,256]{2,1,0:T(2,128)(2,1)S(1)}, u32[]{:S(2)}, u32[]{:S(2)}) %all-to-all-start.3) | async-done | bytes 32800 | tf_op jit(solution)/shard_map/all_to_all | solution.py:47
  174.7 0.7 reshape.260
  175.4 2.7 %all-to-all-start.4 = ((bf16[32,2,256]{2,1,0:T(2,128)(2,1)}), bf16[32,2,256]{2,1,0:T(2,128)(2,1)S(1)}, u32[]{:S(2)}, u32[]{:S(2)}) async-start(bf16[32,2,256]{2,1,0:T(2,128)(2,1)} %reshape.260), calls=%async_computation.4 | async-start | bytes 65536 | tf_op jit(solution)/shard_map/all_to_all | solution.py:58
  178.2 7.1 %all-to-all-done.4 = bf16[32,2,256]{2,1,0:T(2,128)(2,1)S(1)} async-done(((bf16[32,2,256]{2,1,0:T(2,128)(2,1)}), bf16[32,2,256]{2,1,0:T(2,128)(2,1)S(1)}, u32[]{:S(2)}, u32[]{:S(2)}) %all-to-all-start.4) | async-done | bytes 32800 | tf_op jit(solution)/shard_map/all_to_all | solution.py:58
  185.8 0.7 copy-done.8
  186.7 0.7 copy-done.17
  188.3 0.7 reshape.262
  189.0 2.6 %all-to-all-start.5 = ((bf16[32,2,256]{2,1,0:T(2,128)(2,1)}), bf16[32,2,256]{2,1,0:T(2,128)(2,1)S(1)}, u32[]{:S(2)}, u32[]{:S(2)}) async-start(bf16[32,2,256]{2,1,0:T(2,128)(2,1)} %reshape.262), calls=%async_computation.5 | async-start | bytes 65536 | tf_op jit(solution)/shard_map/all_to_all | solution.py:46
  191.7 0.7 reshape.264
  192.5 6.4 %all-to-all-done.5 = bf16[32,2,256]{2,1,0:T(2,128)(2,1)S(1)} async-done(((bf16[32,2,256]{2,1,0:T(2,128)(2,1)}), bf16[32,2,256]{2,1,0:T(2,128)(2,1)S(1)}, u32[]{:S(2)}, u32[]{:S(2)}) %all-to-all-start.5) | async-done | bytes 32800 | tf_op jit(solution)/shard_map/all_to_all | solution.py:46
  198.9 2.6 %all-to-all-start.6 = ((bf16[32,2,256]{2,1,0:T(2,128)(2,1)}), bf16[32,2,256]{2,1,0:T(2,128)(2,1)S(1)}, u32[]{:S(2)}, u32[]{:S(2)}) async-start(bf16[32,2,256]{2,1,0:T(2,128)(2,1)} %reshape.264), calls=%async_computation.6 | async-start | bytes 65536 | tf_op jit(solution)/shard_map/all_to_all | solution.py:47
  201.6 7.0 %all-to-all-done.6 = bf16[32,2,256]{2,1,0:T(2,128)(2,1)S(1)} async-done(((bf16[32,2,256]{2,1,0:T(2,128)(2,1)}), bf16[32,2,256]{2,1,0:T(2,128)(2,1)S(1)}, u32[]{:S(2)}, u32[]{:S(2)}) %all-to-all-start.6) | async-done | bytes 32800 | tf_op jit(solution)/shard_map/all_to_all | solution.py:47
  209.2 0.7 reshape.266
  209.9 2.6 %all-to-all-start.7 = ((bf16[32,2,256]{2,1,0:T(2,128)(2,1)}), bf16[32,2,256]{2,1,0:T(2,128)(2,1)S(1)}, u32[]{:S(2)}, u32[]{:S(2)}) async-start(bf16[32,2,256]{2,1,0:T(2,128)(2,1)} %reshape.266), calls=%async_computation.7 | async-start | bytes 65536 | tf_op jit(solution)/shard_map/all_to_all | solution.py:58
  212.6 0.8 copy.163
  213.3 6.4 %all-to-all-done.7 = bf16[32,2,256]{2,1,0:T(2,128)(2,1)S(1)} async-done(((bf16[32,2,256]{2,1,0:T(2,128)(2,1)}), bf16[32,2,256]{2,1,0:T(2,128)(2,1)S(1)}, u32[]{:S(2)}, u32[]{:S(2)}) %all-to-all-start.7) | async-done | bytes 32800 | tf_op jit(solution)/shard_map/all_to_all | solution.py:58
  220.3 0.9 fusion.15
  (135 shorter events, 11.6 us)
Async XLA Ops:
  0.6 10.8 %copy-start = (bf16[256,768]{1,0:T(8,128)(2,1)S(1)}, bf16[256,768]{1,0:T(8,128)(2,1)}, u32[]{:S(2)}) copy-start(bf16[256,768]{1,0:T(8,128)(2,1)} %param.28) | copy-start | bytes 1179652
  0.6 10.5 %copy-start.1 = (f32[2,64,256]{2,1,0:T(8,128)S(1)}, f32[2,64,256]{2,1,0:T(8,128)}, u32[]{:S(2)}) copy-start(f32[2,64,256]{2,1,0:T(8,128)} %param.22) | copy-start | bytes 393220
  2.2 59.0 %all-to-all-start.1 = ((bf16[2,32,2]{2,0,1:T(2,128)(2,1)}), bf16[2,32,2]{2,0,1:T(2,128)(2,1)S(1)}, u32[]{:S(2)}, u32[]{:S(2)}) async-start(bf16[2,32,2]{2,0,1:T(2,128)(2,1)} %copy.137), calls=%async_computation.1 | async-start | bytes 32768 | tf_op jit(solution)/shard_map/all_to_all | solution.py:163
  11.4 0.7 copy-start.10
  12.3 0.9 copy-start.6
  13.5 0.8 copy-start.2
  14.4 0.7 copy-start.18
  14.6 0.7 copy-start.19
  58.8 0.7 copy-start.13
  58.8 1.4 copy-start.15
  59.5 0.7 copy-start.20
  61.2 44.6 %all-to-all-start = ((bf16[2,64,256]{2,0,1:T(2,128)(2,1)}), bf16[2,64,256]{2,0,1:T(2,128)(2,1)S(1)}, u32[]{:S(2)}, u32[]{:S(2)}) async-start(bf16[2,64,256]{2,0,1:T(2,128)(2,1)} %copy.126), calls=%async_computation | async-start | bytes 131072 | tf_op jit(solution)/shard_map/all_to_all | solution.py:156
  106.3 1.0 copy-start.3
  107.2 0.7 copy-start.11
  108.2 0.9 copy-start.7
  110.5 0.9 copy-start.16
  111.7 0.8 copy-start.9
  111.9 0.7 copy-start.12
  151.5 1.0 copy-start.4
  152.5 0.9 copy-start.5
  154.6 9.8 %all-to-all-start.2 = ((bf16[32,2,256]{2,1,0:T(2,128)(2,1)}), bf16[32,2,256]{2,1,0:T(2,128)(2,1)S(1)}, u32[]{:S(2)}, u32[]{:S(2)}) async-start(bf16[32,2,256]{2,1,0:T(2,128)(2,1)} %reshape.256), calls=%async_computation.2 | async-start | bytes 65536 | tf_op jit(solution)/shard_map/all_to_all | solution.py:46
  164.4 9.8 %all-to-all-start.3 = ((bf16[32,2,256]{2,1,0:T(2,128)(2,1)}), bf16[32,2,256]{2,1,0:T(2,128)(2,1)S(1)}, u32[]{:S(2)}, u32[]{:S(2)}) async-start(bf16[32,2,256]{2,1,0:T(2,128)(2,1)} %reshape.258), calls=%async_computation.3 | async-start | bytes 65536 | tf_op jit(solution)/shard_map/all_to_all | solution.py:47
  175.4 2.7 %copy-start.14 = (f32[2,128]{1,0:T(2,128)S(1)}, f32[2,128]{1,0:T(2,128)}, u32[]{:S(2)}) copy-start(f32[2,128]{1,0:T(2,128)} %param.42) | copy-start | bytes 3076
  175.4 10.0 %all-to-all-start.4 = ((bf16[32,2,256]{2,1,0:T(2,128)(2,1)}), bf16[32,2,256]{2,1,0:T(2,128)(2,1)S(1)}, u32[]{:S(2)}, u32[]{:S(2)}) async-start(bf16[32,2,256]{2,1,0:T(2,128)(2,1)} %reshape.260), calls=%async_computation.4 | async-start | bytes 65536 | tf_op jit(solution)/shard_map/all_to_all | solution.py:58
  185.6 0.8 copy-start.8
  186.5 0.8 copy-start.17
  189.0 9.8 %all-to-all-start.5 = ((bf16[32,2,256]{2,1,0:T(2,128)(2,1)}), bf16[32,2,256]{2,1,0:T(2,128)(2,1)S(1)}, u32[]{:S(2)}, u32[]{:S(2)}) async-start(bf16[32,2,256]{2,1,0:T(2,128)(2,1)} %reshape.262), calls=%async_computation.5 | async-start | bytes 65536 | tf_op jit(solution)/shard_map/all_to_all | solution.py:46
  198.9 9.8 %all-to-all-start.6 = ((bf16[32,2,256]{2,1,0:T(2,128)(2,1)}), bf16[32,2,256]{2,1,0:T(2,128)(2,1)S(1)}, u32[]{:S(2)}, u32[]{:S(2)}) async-start(bf16[32,2,256]{2,1,0:T(2,128)(2,1)} %reshape.264), calls=%async_computation.6 | async-start | bytes 65536 | tf_op jit(solution)/shard_map/all_to_all | solution.py:47
  209.9 9.8 %all-to-all-start.7 = ((bf16[32,2,256]{2,1,0:T(2,128)(2,1)}), bf16[32,2,256]{2,1,0:T(2,128)(2,1)S(1)}, u32[]{:S(2)}, u32[]{:S(2)}) async-start(bf16[32,2,256]{2,1,0:T(2,128)(2,1)} %reshape.266), calls=%async_computation.7 | async-start | bytes 65536 | tf_op jit(solution)/shard_map/all_to_all | solution.py:58
where the time goes:
time: 222 us; the launch traced here: 221 us
  blocking collectives  122 us (55%)
  waiting for transfers between devices  40.4 us (18%)
  starting transfers between devices  25.4 us (11%)
  local copies, waits for them, and re-layouts  20.1 us (9%)
  matrix products  7.19 us (3%)
  other arithmetic  4.68 us (2%)
    all_gather x1, blocking collectives, shards(): bias_whole = lax.all_gather(bias_local, 'dap', axis=1, tiled=True)  42.1 us
    all_gather x1, blocking collectives, shards(): lax.all_gather(col_mask.astype(jnp.bfloat16), 'dap', axis=1, tiled=True)  41.8 us
    all_gather x1, blocking collectives, shards(): lax.all_gather(right_proj, 'dap', axis=1, tiled=True)  38.1 us
    unnamed x55, local copies, waits for them, and re-layouts  15 us
    all_to_all x2, waiting for transfers between devices, triangle(): lax.all_to_all(right_side, 'dap', split_axis=0, concat_axis=1, tiled=True)  14.1 us
    all_to_all x2, waiting for transfers between devices, triangle(): lax.all_to_all(product, 'dap', split_axis=1, concat_axis=0, tiled=True)  13.5 us
    all_to_all x2, waiting for transfers between devices, triangle(): lax.all_to_all(left_side, 'dap', split_axis=0, concat_axis=1, tiled=True)  12.8 us
    all_to_all x1, starting transfers between devices, shards(): lax.all_to_all(homolog_presence.astype(jnp.float32).astype(jnp.bfloat16),...  7.33 us
  transfers between devices with their start and end apart: 8, of which 6 were waited for; matrix products, arithmetic and copies ran while one was open for 4% of the time, Pallas kernels for 0%

commit v1 on v0

--- a/solution.py
+++ b/solution.py
@@ -10,6 +10,14 @@
 TRI_HID = 128
 EPSILON = 1e-05
 MASK_PENALTY_SCALE = 1000000000.0
+
+
+def tiled_gather(array, axis, dim):
+    size = lax.axis_size(axis)
+    repeats = [size if d == dim else 1 for d in range(array.ndim)]
+    return lax.all_to_all(
+        jnp.tile(array, repeats), axis, split_axis=dim, concat_axis=dim, tiled=True
+    )
 
 
 def standardize_features(content_vectors, gain, axis):
@@ -215,7 +223,7 @@
     right_proj = (halves[..., TENSOR_HIDDEN:] * col_mask[..., None]).astype(jnp.bfloat16)
     right_whole, mask_whole = (
         lax.all_gather(right_proj, "dap", axis=1, tiled=True),
-        lax.all_gather(col_mask.astype(jnp.bfloat16), "dap", axis=1, tiled=True),
+        tiled_gather(col_mask.astype(jnp.bfloat16), "dap", 1),
     )
     outer = jnp.einsum("sra,sjb->rjab", left_proj, right_whole, preferred_element_type=jnp.float32)
     outer = outer.astype(jnp.bfloat16).reshape(

time: 222 us -> 198 us (0.89)
  blocking collectives: 122 us -> 80.7 us
  waiting for transfers between devices: 40.4 us -> 54.7 us
  starting transfers between devices: 25.4 us -> 28 us
    all_gather x1 -> x0, blocking collectives: 41.8 us -> none  [shards(): lax.all_gather(col_mask.astype(jnp.bfloat16), 'dap', axis=1, tiled=True)]
    all_to_all x1, waiting for transfers between devices: 0.01 us -> 7.23 us  [shards(): lax.all_to_all(homolog_stack_horizontal.astype(jnp.bfloat16), 'dap', spli...]
    all_to_all x0 -> x1, waiting for transfers between devices: none -> 7.08 us  [tiled_gather(): lax.all_to_all(jnp.tile(array, repeats), axis, split_axis=dim, concat_axi...]
    all_to_all x0 -> x1, starting transfers between devices: none -> 2.54 us  [tiled_gather(): lax.all_to_all(jnp.tile(array, repeats), axis, split_axis=dim, concat_axi...]
  transfers between devices with their start and end apart: 8 -> 9, of which waited for: 6 -> 8; matrix products, arithmetic and copies ran while one was open for 4% -> 4% of each run, Pallas kernels for 0% -> 0%
where the time goes in v1:
time: 198 us; the launch traced here: 197 us
  blocking collectives  80.7 us (41%)
  waiting for transfers between devices  54.7 us (28%)
  starting transfers between devices  28 us (14%)
  local copies, waits for them, and re-layouts  20.8 us (11%)
  matrix products  7.2 us (4%)
  other arithmetic  4.67 us (2%)
    all_gather x1, blocking collectives, shards(): bias_whole = lax.all_gather(bias_local, 'dap', axis=1, tiled=True)  42.1 us
    all_gather x1, blocking collectives, shards(): lax.all_gather(right_proj, 'dap', axis=1, tiled=True)  38.6 us
    unnamed x55, local copies, waits for them, and re-layouts  15 us
    all_to_all x2, waiting for transfers between devices, triangle(): lax.all_to_all(right_side, 'dap', split_axis=0, concat_axis=1, tiled=True)  14.1 us
    all_to_all x2, waiting for transfers between devices, triangle(): lax.all_to_all(product, 'dap', split_axis=1, concat_axis=0, tiled=True)  13.5 us
    all_to_all x2, waiting for transfers between devices, triangle(): lax.all_to_all(left_side, 'dap', split_axis=0, concat_axis=1, tiled=True)  12.8 us
    all_to_all x1, starting transfers between devices, shards(): lax.all_to_all(homolog_presence.astype(jnp.float32).astype(jnp.bfloat16),...  7.33 us
    all_to_all x1, waiting for transfers between devices, shards(): lax.all_to_all(homolog_stack_horizontal.astype(jnp.bfloat16), 'dap', spli...  7.23 us
  transfers between devices with their start and end apart: 9, of which 8 were waited for; matrix products, arithmetic and copies ran while one was open for 4% of the time, Pallas kernels for 0%

profile of v1, /device:TPU:0, one launch (start us, length us, event | category | flops | bytes accessed | tf_op | source)
XLA Modules:
  0.0 197.4 jit_solution(9561489988238035967)
XLA Ops:
  0.7 0.8 convert_convert_fusion
  1.5 0.6 copy.138
  2.2 7.3 %all-to-all-start.1 = ((bf16[2,32,2]{2,0,1:T(2,128)(2,1)}), bf16[2,32,2]{2,0,1:T(2,128)(2,1)S(1)}, u32[]{:S(2)}, u32[]{:S(2)}) async-start(bf16[2,32,2]{2,0,1:T(2,128)(2,1)} %copy.138), calls=%async_computation.1 | async-start | bytes 32768 | tf_op jit(solution)/shard_map/all_to_all | solution.py:171
  9.5 0.7 add_multiply_fusion
  10.2 1.0 reduce_sum.163
  11.4 0.7 copy-done.10
  12.5 0.8 copy-done.6
  13.6 0.7 copy-done.2
  14.6 0.5 copy-done.18
  15.5 42.1 %all_gather.6 = bf16[8,64,64]{2,0,1:T(8,128)(2,1)S(1)} all-gather(bf16[8,2,64]{2,0,1:T(8,128)(2,1)S(1)} %fusion.22), channel_id=1, replica_groups=mesh['dap'=32] {'dap'}, dimensions={1}, use_global_device_ids=true | all-gather | bytes 67584 | tf_op jit(solution)/shard_map/all_gather | solution.py:148
  58.0 0.4 fusion.118
  58.9 0.5 copy-done.13
  59.5 0.7 copy-done.20
  60.5 0.7 copy.127
  61.2 0.6 tile.2
  61.9 2.5 %all-to-all-start.2 = ((bf16[64,32,2]{0,2,1:T(2,128)(2,1)}), bf16[64,32,2]{0,2,1:T(2,128)(2,1)S(1)}, u32[]{:S(2)}, u32[]{:S(2)}) async-start(bf16[64,32,2]{0,2,1:T(2,128)(2,1)} %tile.2), calls=%async_computation.2 | async-start | bytes 32768 | tf_op jit(solution)/shard_map/all_to_all | solution.py:18
  64.5 7.1 %all-to-all-done.2 = bf16[64,32,2]{0,2,1:T(2,128)(2,1)S(1)} async-done(((bf16[64,32,2]{0,2,1:T(2,128)(2,1)}), bf16[64,32,2]{0,2,1:T(2,128)(2,1)S(1)}, u32[]{:S(2)}, u32[]{:S(2)}) %all-to-all-start.2) | async-done | bytes 8224 | tf_op jit(solution)/shard_map/all_to_all | solution.py:18
  71.5 2.6 %all-to-all-start = ((bf16[2,64,256]{2,0,1:T(2,128)(2,1)}), bf16[2,64,256]{2,0,1:T(2,128)(2,1)S(1)}, u32[]{:S(2)}, u32[]{:S(2)}) async-start(bf16[2,64,256]{2,0,1:T(2,128)(2,1)} %copy.127), calls=%async_computation | async-start | bytes 131072 | tf_op jit(solution)/shard_map/all_to_all | solution.py:164
  74.3 7.2 %all-to-all-done = bf16[2,64,256]{2,0,1:T(2,128)(2,1)S(1)} async-done(((bf16[2,64,256]{2,0,1:T(2,128)(2,1)}), bf16[2,64,256]{2,0,1:T(2,128)(2,1)S(1)}, u32[]{:S(2)}, u32[]{:S(2)}) %all-to-all-start) | async-done | bytes 65568 | tf_op jit(solution)/shard_map/all_to_all | solution.py:164
  83.0 0.6 copy-done.11
  84.0 0.8 copy-done.7
  86.3 0.8 copy-done.16
  87.6 0.6 copy-done.9
  88.5 38.6 %all_gather.7 = bf16[64,64,32]{0,2,1:T(8,128)(2,1)S(1)} all-gather(bf16[64,2,32]{0,2,1:T(8,128)(2,1)S(1)} %fusion.80), channel_id=1, replica_groups=mesh['dap'=32] {'dap'}, dimensions={1}, use_global_device_ids=true | all-gather | bytes 270336 | tf_op jit(solution)/shard_map/all_gather | solution.py:225
  127.1 0.6 fusion.6
  128.1 0.6 copy-done.4
  130.1 0.7 reshape.262
  130.9 2.6 %all-to-all-start.3 = ((bf16[32,2,256]{2,1,0:T(2,128)(2,1)}), bf16[32,2,256]{2,1,0:T(2,128)(2,1)S(1)}, u32[]{:S(2)}, u32[]{:S(2)}) async-start(bf16[32,2,256]{2,1,0:T(2,128)(2,1)} %reshape.262), calls=%async_computation.3 | async-start | bytes 65536 | tf_op jit(solution)/shard_map/all_to_all | solution.py:54
  133.6 0.7 reshape.264
  134.3 6.4 %all-to-all-done.3 = bf16[32,2,256]{2,1,0:T(2,128)(2,1)S(1)} async-done(((bf16[32,2,256]{2,1,0:T(2,128)(2,1)}), bf16[32,2,256]{2,1,0:T(2,128)(2,1)S(1)}, u32[]{:S(2)}, u32[]{:S(2)}) %all-to-all-start.3) | async-done | bytes 32800 | tf_op jit(solution)/shard_map/all_to_all | solution.py:54
  140.7 2.6 %all-to-all-start.4 = ((bf16[32,2,256]{2,1,0:T(2,128)(2,1)}), bf16[32,2,256]{2,1,0:T(2,128)(2,1)S(1)}, u32[]{:S(2)}, u32[]{:S(2)}) async-start(bf16[32,2,256]{2,1,0:T(2,128)(2,1)} %reshape.264), calls=%async_computation.4 | async-start | bytes 65536 | tf_op jit(solution)/shard_map/all_to_all | solution.py:55
  143.5 7.0 %all-to-all-done.4 = bf16[32,2,256]{2,1,0:T(2,128)(2,1)S(1)} async-done(((bf16[32,2,256]{2,1,0:T(2,128)(2,1)}), bf16[32,2,256]{2,1,0:T(2,128)(2,1)S(1)}, u32[]{:S(2)}, u32[]{:S(2)}) %all-to-all-start.4) | async-done | bytes 32800 | tf_op jit(solution)/shard_map/all_to_all | solution.py:55
  151.0 0.7 reshape.266
  151.7 2.7 %all-to-all-start.5 = ((bf16[32,2,256]{2,1,0:T(2,128)(2,1)}), bf16[32,2,256]{2,1,0:T(2,128)(2,1)S(1)}, u32[]{:S(2)}, u32[]{:S(2)}) async-start(bf16[32,2,256]{2,1,0:T(2,128)(2,1)} %reshape.266), calls=%async_computation.5 | async-start | bytes 65536 | tf_op jit(solution)/shard_map/all_to_all | solution.py:66
  154.5 7.1 %all-to-all-done.5 = bf16[32,2,256]{2,1,0:T(2,128)(2,1)S(1)} async-done(((bf16[32,2,256]{2,1,0:T(2,128)(2,1)}), bf16[32,2,256]{2,1,0:T(2,128)(2,1)S(1)}, u32[]{:S(2)}, u32[]{:S(2)}) %all-to-all-start.5) | async-done | bytes 32800 | tf_op jit(solution)/shard_map/all_to_all | solution.py:66
  162.0 0.7 copy-done.8
  162.9 0.7 copy-done.17
  164.6 0.7 reshape.268
  165.3 2.6 %all-to-all-start.6 = ((bf16[32,2,256]{2,1,0:T(2,128)(2,1)}), bf16[32,2,256]{2,1,0:T(2,128)(2,1)S(1)}, u32[]{:S(2)}, u32[]{:S(2)}) async-start(bf16[32,2,256]{2,1,0:T(2,128)(2,1)} %reshape.268), calls=%async_computation.6 | async-start | bytes 65536 | tf_op jit(solution)/shard_map/all_to_all | solution.py:54
  168.0 0.7 reshape.270
  168.7 6.4 %all-to-all-done.6 = bf16[32,2,256]{2,1,0:T(2,128)(2,1)S(1)} async-done(((bf16[32,2,256]{2,1,0:T(2,128)(2,1)}), bf16[32,2,256]{2,1,0:T(2,128)(2,1)S(1)}, u32[]{:S(2)}, u32[]{:S(2)}) %all-to-all-start.6) | async-done | bytes 32800 | tf_op jit(solution)/shard_map/all_to_all | solution.py:54
  175.1 2.6 %all-to-all-start.7 = ((bf16[32,2,256]{2,1,0:T(2,128)(2,1)}), bf16[32,2,256]{2,1,0:T(2,128)(2,1)S(1)}, u32[]{:S(2)}, u32[]{:S(2)}) async-start(bf16[32,2,256]{2,1,0:T(2,128)(2,1)} %reshape.270), calls=%async_computation.7 | async-start | bytes 65536 | tf_op jit(solution)/shard_map/all_to_all | solution.py:55
  177.9 7.0 %all-to-all-done.7 = bf16[32,2,256]{2,1,0:T(2,128)(2,1)S(1)} async-done(((bf16[32,2,256]{2,1,0:T(2,128)(2,1)}), bf16[32,2,256]{2,1,0:T(2,128)(2,1)S(1)}, u32[]{:S(2)}, u32[]{:S(2)}) %all-to-all-start.7) | async-done | bytes 32800 | tf_op jit(solution)/shard_map/all_to_all | solution.py:55
  185.4 0.7 reshape.272
  186.2 2.6 %all-to-all-start.8 = ((bf16[32,2,256]{2,1,0:T(2,128)(2,1)}), bf16[32,2,256]{2,1,0:T(2,128)(2,1)S(1)}, u32[]{:S(2)}, u32[]{:S(2)}) async-start(bf16[32,2,256]{2,1,0:T(2,128)(2,1)} %reshape.272), calls=%async_computation.8 | async-start | bytes 65536 | tf_op jit(solution)/shard_map/all_to_all | solution.py:66
  188.9 0.8 copy.164
  189.6 6.4 %all-to-all-done.8 = bf16[32,2,256]{2,1,0:T(2,128)(2,1)S(1)} async-done(((bf16[32,2,256]{2,1,0:T(2,128)(2,1)}), bf16[32,2,256]{2,1,0:T(2,128)(2,1)S(1)}, u32[]{:S(2)}, u32[]{:S(2)}) %all-to-all-start.8) | async-done | bytes 32800 | tf_op jit(solution)/shard_map/all_to_all | solution.py:66
  196.6 0.9 fusion.15
  (137 shorter events, 12.7 us)
Async XLA Ops:
  0.6 10.8 %copy-start = (bf16[256,768]{1,0:T(8,128)(2,1)S(1)}, bf16[256,768]{1,0:T(8,128)(2,1)}, u32[]{:S(2)}) copy-start(bf16[256,768]{1,0:T(8,128)(2,1)} %param.28) | copy-start | bytes 1179652
  0.6 10.5 %copy-start.1 = (f32[2,64,256]{2,1,0:T(8,128)S(1)}, f32[2,64,256]{2,1,0:T(8,128)}, u32[]{:S(2)}) copy-start(f32[2,64,256]{2,1,0:T(8,128)} %param.22) | copy-start | bytes 393220
  2.2 59.0 %all-to-all-start.1 = ((bf16[2,32,2]{2,0,1:T(2,128)(2,1)}), bf16[2,32,2]{2,0,1:T(2,128)(2,1)S(1)}, u32[]{:S(2)}, u32[]{:S(2)}) async-start(bf16[2,32,2]{2,0,1:T(2,128)(2,1)} %copy.138), calls=%async_computation.1 | async-start | bytes 32768 | tf_op jit(solution)/shard_map/all_to_all | solution.py:171
  11.4 0.7 copy-start.10
  12.3 0.9 copy-start.6
  13.5 0.8 copy-start.2
  14.4 0.7 copy-start.18
  14.6 0.7 copy-start.19
  58.8 0.7 copy-start.13
  58.8 1.4 copy-start.15
  59.5 0.7 copy-start.20
  61.9 9.7 %all-to-all-start.2 = ((bf16[64,32,2]{0,2,1:T(2,128)(2,1)}), bf16[64,32,2]{0,2,1:T(2,128)(2,1)S(1)}, u32[]{:S(2)}, u32[]{:S(2)}) async-start(bf16[64,32,2]{0,2,1:T(2,128)(2,1)} %tile.2), calls=%async_computation.2 | async-start | bytes 32768 | tf_op jit(solution)/shard_map/all_to_all | solution.py:18
  71.5 10.0 %all-to-all-start = ((bf16[2,64,256]{2,0,1:T(2,128)(2,1)}), bf16[2,64,256]{2,0,1:T(2,128)(2,1)S(1)}, u32[]{:S(2)}, u32[]{:S(2)}) async-start(bf16[2,64,256]{2,0,1:T(2,128)(2,1)} %copy.127), calls=%async_computation | async-start | bytes 131072 | tf_op jit(solution)/shard_map/all_to_all | solution.py:164
  82.0 1.0 copy-start.3
  82.9 0.7 copy-start.11
  83.9 0.9 copy-start.7
  86.2 0.9 copy-start.16
  87.4 0.8 copy-start.9
  87.6 0.7 copy-start.12
  127.8 1.0 copy-start.4
  128.7 0.9 copy-start.5
  130.9 9.8 %all-to-all-start.3 = ((bf16[32,2,256]{2,1,0:T(2,128)(2,1)}), bf16[32,2,256]{2,1,0:T(2,128)(2,1)S(1)}, u32[]{:S(2)}, u32[]{:S(2)}) async-start(bf16[32,2,256]{2,1,0:T(2,128)(2,1)} %reshape.262), calls=%async_computation.3 | async-start | bytes 65536 | tf_op jit(solution)/shard_map/all_to_all | solution.py:54
  140.7 9.8 %all-to-all-start.4 = ((bf16[32,2,256]{2,1,0:T(2,128)(2,1)}), bf16[32,2,256]{2,1,0:T(2,128)(2,1)S(1)}, u32[]{:S(2)}, u32[]{:S(2)}) async-start(bf16[32,2,256]{2,1,0:T(2,128)(2,1)} %reshape.264), calls=%async_computation.4 | async-start | bytes 65536 | tf_op jit(solution)/shard_map/all_to_all | solution.py:55
  151.7 2.7 %copy-start.14 = (f32[2,128]{1,0:T(2,128)S(1)}, f32[2,128]{1,0:T(2,128)}, u32[]{:S(2)}) copy-start(f32[2,128]{1,0:T(2,128)} %param.42) | copy-start | bytes 3076
  151.7 10.0 %all-to-all-start.5 = ((bf16[32,2,256]{2,1,0:T(2,128)(2,1)}), bf16[32,2,256]{2,1,0:T(2,128)(2,1)S(1)}, u32[]{:S(2)}, u32[]{:S(2)}) async-start(bf16[32,2,256]{2,1,0:T(2,128)(2,1)} %reshape.266), calls=%async_computation.5 | async-start | bytes 65536 | tf_op jit(solution)/shard_map/all_to_all | solution.py:66
  161.9 0.8 copy-start.8
  162.8 0.8 copy-start.17
  165.3 9.8 %all-to-all-start.6 = ((bf16[32,2,256]{2,1,0:T(2,128)(2,1)}), bf16[32,2,256]{2,1,0:T(2,128)(2,1)S(1)}, u32[]{:S(2)}, u32[]{:S(2)}) async-start(bf16[32,2,256]{2,1,0:T(2,128)(2,1)} %reshape.268), calls=%async_computation.6 | async-start | bytes 65536 | tf_op jit(solution)/shard_map/all_to_all | solution.py:54
  175.1 9.8 %all-to-all-start.7 = ((bf16[32,2,256]{2,1,0:T(2,128)(2,1)}), bf16[32,2,256]{2,1,0:T(2,128)(2,1)S(1)}, u32[]{:S(2)}, u32[]{:S(2)}) async-start(bf16[32,2,256]{2,1,0:T(2,128)(2,1)} %reshape.270), calls=%async_computation.7 | async-start | bytes 65536 | tf_op jit(solution)/shard_map/all_to_all | solution.py:55
  186.2 9.8 %all-to-all-start.8 = ((bf16[32,2,256]{2,1,0:T(2,128)(2,1)}), bf16[32,2,256]{2,1,0:T(2,128)(2,1)S(1)}, u32[]{:S(2)}, u32[]{:S(2)}) async-start(bf16[32,2,256]{2,1,0:T(2,128)(2,1)} %reshape.272), calls=%async_computation.8 | async-start | bytes 65536 | tf_op jit(solution)/shard_map/all_to_all | solution.py:66
